TPU v7x, 32 devices: a whole 2x2x4 slice. The times are simulated.
32 devices in a mesh: col: 8 (over z, y), lev: 4 (over x, core).
Axes of the slice: x: 2, y: 2, z: 4, core: 2. Of those that a mesh axis runs over, the one named last changes fastest.
Arguments:
- state_anom: bfloat16 [48, 64, 8192], P('lev', None, 'col'), may hold values from -6 to 6
- error_sum: float32 [48, 8192], P('lev', 'col'), may hold values from -3 to 3
- obs_anom: bfloat16 [64, 16384], P('lev', 'col'), may hold values from -6 to 6
- local_weight: float32 [32, 16384], P(None, 'col'), may hold values from 0.05 to 1
- neighbours: int32 [32, 16384], P(None, 'col'), may hold values from 0 to 3071, as said below
- innovation: float32 [16384], P(('col', 'lev')), may hold values from -6 to 6
- obs_type: int32 [16384], P(('col', 'lev')), may hold values from 0 to 31
- live: int32 [16384], P(('col', 'lev')), may hold values 0 or 1
Outputs:
- impact: float32 [16384], P(('col', 'lev'))
- type_impact: float32 [32], replicated
Inputs may be any that keep to these rules, and one draw needn't show every extreme that they name: Observation o lies in column tile o // 2048; the column (o // 2048 - 1) * 1024 + neighbours[n, o] lies in that tile or the tile on either side of it, inside the grid.
All inputs are finite; a program needn't handle non-finite values. No bound on the sum of `live` on one device may be relied on, other than what follows from the above.
Results may differ from a plain program's by a relative error of at most 0.0003.
Values may be sent and summed in bfloat16 or wider, within the bound.
A program may use at most 64 MiB of HBM per device.

v0:
```python
import math
import jax
import jax.numpy as jnp
from jax import lax
from jax.sharding import PartitionSpec as P

MEMBERS = 64
NTYPE = 32


def with_halo(cells, sides, width):
    for axis, dim in sides:
        count = lax.axis_size(axis)
        ends = count - 1
        head = lax.slice_in_dim(cells, 0, width, axis=dim)
        tail = lax.slice_in_dim(cells, cells.shape[dim] - width, cells.shape[dim], axis=dim)
        cells = jnp.concatenate(
            [
                lax.ppermute(tail, axis, [(i, (i + 1) % count) for i in range(ends)]),
                cells,
                lax.ppermute(head, axis, [((i + 1) % count, i) for i in range(ends)]),
            ],
            axis=dim,
        )
    return cells


def block_pairs(extended, anom, weight, index):
    span = extended.shape[1]
    column_ids = lax.broadcasted_iota(jnp.int32, (span, index.shape[1]), 0)
    table = jnp.sum(
        jnp.where(index[:, None, :] == column_ids[None, :, :], weight[:, None, :], 0.0), axis=0
    )
    spread = jnp.dot(
        extended, table, precision=lax.Precision.HIGHEST, preferred_element_type=jnp.float32
    )
    return jnp.sum(anom.astype(jnp.float32) * spread, axis=0)


def shards(state_anom, error_sum, obs_anom, local_weight, neighbours, innovation, obs_type, live):
    columns = state_anom.shape[2]
    regrouped = lax.all_to_all(state_anom, "lev", split_axis=1, concat_axis=0, tiled=True)
    all_error = lax.all_gather(error_sum, "lev", axis=0, tiled=True)
    sens = jnp.einsum(
        "lkc,lc->kc", regrouped.astype(jnp.float32), all_error, precision=lax.Precision.HIGHEST
    )
    extended = with_halo(sens, (("col", 1),), columns)
    obs_slots = obs_anom.shape[1]
    step_rows = math.gcd(obs_slots, 512)
    count = obs_slots // step_rows
    groups = obs_anom.shape[0]
    anom_blocks = jnp.transpose(obs_anom.reshape(groups, count, step_rows), (1, 0, 2))
    weight_blocks = jnp.transpose(
        local_weight.reshape(local_weight.shape[0], count, step_rows), (1, 0, 2)
    )
    index_blocks = jnp.transpose(
        neighbours.reshape(neighbours.shape[0], count, step_rows), (1, 0, 2)
    )

    def one_block(items):
        return block_pairs(extended, items[0], items[1], items[2])

    partial_pair = lax.map(one_block, (anom_blocks, weight_blocks, index_blocks)).reshape(obs_slots)
    pair = lax.psum_scatter(partial_pair, "lev", scatter_dimension=0, tiled=True)
    impact = pair * innovation * live.astype(jnp.float32) / (MEMBERS - 1.0)
    onehot = (obs_type[None, :] == jnp.arange(NTYPE, dtype=jnp.int32)[:, None]).astype(jnp.float32)
    type_part = jnp.sum(onehot * impact[None, :], axis=1)
    type_impact = lax.psum(type_part, ("col", "lev"))
    return (impact, type_impact)


def solution(mesh):
    in_specs = (
        P("lev", None, "col"),
        P("lev", "col"),
        P("lev", "col"),
        P(None, "col"),
        P(None, "col"),
        P(("col", "lev")),
        P(("col", "lev")),
        P(("col", "lev")),
    )
    out_specs = (P(("col", "lev")), P())
    return jax.shard_map(shards, mesh=mesh, in_specs=in_specs, out_specs=out_specs, check_vma=False)
```

profile of v0, /device:TPU:0, one launch (start us, length us, event | category | flops | bytes accessed | tf_op | source)
XLA Modules:
  0.0 241.2 jit_solution(3400720630463568245)
XLA Ops:
  0.6 0.0 copy-start.2
  0.6 0.0 copy-start
  0.6 3.7 %copy.23 = bf16[12,64,1024]{2,0,1:T(8,128)(2,1)} copy(bf16[12,64,1024]{2,1,0:T(8,128)(2,1)} %param.10) | data formatting | bytes 3145728 | tf_op args[0]
  4.4 0.0 copy-start.1
  4.4 0.0 copy-start.3
  4.4 0.0 copy-start.8
  4.4 4.4 %all-to-all-start = ((bf16[12,64,1024]{2,0,1:T(8,128)(2,1)}), bf16[12,64,1024]{2,0,1:T(8,128)(2,1)S(1)}, u32[]{:S(2)}, u32[]{:S(2)}) async-start(bf16[12,64,1024]{2,0,1:T(8,128)(2,1)} %copy.23), calls=%async_computation | async-start | bytes 4194304 | tf_op jit(solution)/shard_map/all_to_all | solution.py:42
  8.7 0.0 copy-done.2
  8.7 27.9 %all-gather = f32[4,12,1024]{2,1,0:T(8,128)S(1)} all-gather(f32[1,12,1024]{2,1,0:T(8,128)S(1)} %bitcast.60), channel_id=1, replica_groups=mesh['col'=8,'lev'=4] {'lev'}, dimensions={0}, use_global_device_ids=true | all-gather | bytes 245760 | tf_op jit(solution)/shard_map/all_gather | solution.py:43
  36.7 0.0 all-to-all-done
  36.7 0.9 copy.36
  37.6 0.4 multiply_reduce_fusion
  38.0 4.2 %collective-permute-start = (f32[16,1024]{1,0:T(8,128)S(1)}, f32[16,1024]{1,0:T(8,128)S(1)}, u32[]{:S(2)}, u32[]{:S(2)}) collective-permute-start(f32[16,1024]{1,0:T(8,128)S(1)} %bitcast.55), channel_id=1, source_target_pairs={{0,4},{4,8},{8,12},{12,16},{16,20},{20,24},{24,28},{1,5},{5,9},{9,... | collective-permute-start | bytes 196616 | tf_op jit(solution)/shard_map/ppermute | solution.py:19
  42.3 1.3 collective-permute-start.1
  43.6 0.0 copy-done
  43.6 0.2 reshape.25
  43.8 0.0 copy-done.1
  43.8 0.2 reshape.26
  43.9 0.0 copy-done.3
  44.0 0.0 copy-done.8
  44.0 0.6 dynamic-slice
  45.3 0.0 collective-permute-done
  45.3 3.1 %collective-permute-done.1 = f32[16,1024]{1,0:T(8,128)S(1)} collective-permute-done((f32[16,1024]{1,0:T(8,128)S(1)}, f32[16,1024]{1,0:T(8,128)S(1)}, u32[]{:S(2)}, u32[]{:S(2)}) %collective-permute-start.1) | collective-permute-done | bytes 65568 | tf_op jit(solution)/shard_map/ppermute | solution.py:21
  48.4 0.0 copy-start.5
  48.4 0.0 copy-start.6
  48.5 0.0 copy-start.7
  48.5 146.3 %while.10 = (s32[]{:T(128)}, f32[4,512]{1,0:T(4,128)S(1)}, bf16[4,16,512]{2,1,0:T(8,128)(2,1)S(1)}, s32[4,32,512]{2,0,1:T(4,128)S(1)}, f32[4,32,512]{2,0,1:T(4,1...) while((s32[]{:T(128)}, f32[4,512]{1,0:T(4,128)S(1)}, bf16[4,16,512]{2,1,0:T(8,128)(2,1)S(1)}, ...), condition=%wide.region_3.4_spmd, body=%wide.region_0.3_spmd.sunk | while | flops 451436032 | bytes 13457509 | solution.py:63
  48.5 0.1 constant_dynamic-slice_fusion.4
  48.6 0.1 constant_dynamic-slice_fusion.5
  48.6 30.9 %select_reduce_fusion.3 = f32[3072,512]{1,0:T(8,128)} fusion(f32[32,512]{1,0:T(8,128)S(1)} %bitcast.50, s32[32,512]{1,0:T(8,128)S(1)} %bitcast.51), kind=kLoop, calls=%fused_computation.clone.1 | loop fusion | flops 149422080 | bytes 6422528 | tf_op jit(solution)/shard_map/while/body/eval_jaxpr/reduce_sum | solution.py:31
  79.6 5.4 %fusion.11 = f32[512]{0:T(512)S(1)} fusion(f32[3072,512]{1,0:T(8,128)} %select_reduce_fusion.3, f32[16,3072]{1,0:T(8,128)S(1)} %get-tuple-element.129, bf16[4,16,512]{2,1,0:T(8,128)(2,1)S(1)} %get-tuple-element.126, s32[]{:T(128)} %get-tuple-element.116), kind=kOutput, calls=%fused_computation.4.clone.1 | convolution fusion | flops 302013952 | bytes 6506500 | tf_op jit(solution)/shard_map/while/body/eval_jaxpr/dot_general | solution.py:34
  85.0 0.1 dynamic_update_slice.5
  85.0 0.1 constant_dynamic-slice_fusion.4
  85.1 0.1 constant_dynamic-slice_fusion.5
  85.2 30.9 %select_reduce_fusion.3 = f32[3072,512]{1,0:T(8,128)} fusion(f32[32,512]{1,0:T(8,128)S(1)} %bitcast.50, s32[32,512]{1,0:T(8,128)S(1)} %bitcast.51), kind=kLoop, calls=%fused_computation.clone.1 | loop fusion | flops 149422080 | bytes 6422528 | tf_op jit(solution)/shard_map/while/body/eval_jaxpr/reduce_sum | solution.py:31
  116.1 5.4 %fusion.11 = f32[512]{0:T(512)S(1)} fusion(f32[3072,512]{1,0:T(8,128)} %select_reduce_fusion.3, f32[16,3072]{1,0:T(8,128)S(1)} %get-tuple-element.129, bf16[4,16,512]{2,1,0:T(8,128)(2,1)S(1)} %get-tuple-element.126, s32[]{:T(128)} %get-tuple-element.116), kind=kOutput, calls=%fused_computation.4.clone.1 | convolution fusion | flops 302013952 | bytes 6506500 | tf_op jit(solution)/shard_map/while/body/eval_jaxpr/dot_general | solution.py:34
  121.5 0.1 dynamic_update_slice.5
  121.6 0.1 constant_dynamic-slice_fusion.4
  121.7 0.1 constant_dynamic-slice_fusion.5
  121.8 30.9 %select_reduce_fusion.3 = f32[3072,512]{1,0:T(8,128)} fusion(f32[32,512]{1,0:T(8,128)S(1)} %bitcast.50, s32[32,512]{1,0:T(8,128)S(1)} %bitcast.51), kind=kLoop, calls=%fused_computation.clone.1 | loop fusion | flops 149422080 | bytes 6422528 | tf_op jit(solution)/shard_map/while/body/eval_jaxpr/reduce_sum | solution.py:31
  152.7 5.4 %fusion.11 = f32[512]{0:T(512)S(1)} fusion(f32[3072,512]{1,0:T(8,128)} %select_reduce_fusion.3, f32[16,3072]{1,0:T(8,128)S(1)} %get-tuple-element.129, bf16[4,16,512]{2,1,0:T(8,128)(2,1)S(1)} %get-tuple-element.126, s32[]{:T(128)} %get-tuple-element.116), kind=kOutput, calls=%fused_computation.4.clone.1 | convolution fusion | flops 302013952 | bytes 6506500 | tf_op jit(solution)/shard_map/while/body/eval_jaxpr/dot_general | solution.py:34
  158.1 0.1 dynamic_update_slice.5
  158.2 0.1 constant_dynamic-slice_fusion.4
  158.3 0.1 constant_dynamic-slice_fusion.5
  158.4 30.9 %select_reduce_fusion.3 = f32[3072,512]{1,0:T(8,128)} fusion(f32[32,512]{1,0:T(8,128)S(1)} %bitcast.50, s32[32,512]{1,0:T(8,128)S(1)} %bitcast.51), kind=kLoop, calls=%fused_computation.clone.1 | loop fusion | flops 149422080 | bytes 6422528 | tf_op jit(solution)/shard_map/while/body/eval_jaxpr/reduce_sum | solution.py:31
  189.3 5.4 %fusion.11 = f32[512]{0:T(512)S(1)} fusion(f32[3072,512]{1,0:T(8,128)} %select_reduce_fusion.3, f32[16,3072]{1,0:T(8,128)S(1)} %get-tuple-element.129, bf16[4,16,512]{2,1,0:T(8,128)(2,1)S(1)} %get-tuple-element.126, s32[]{:T(128)} %get-tuple-element.116), kind=kOutput, calls=%fused_computation.4.clone.1 | convolution fusion | flops 302013952 | bytes 6506500 | tf_op jit(solution)/shard_map/while/body/eval_jaxpr/dot_general | solution.py:34
  194.7 0.1 dynamic_update_slice.5
  194.8 5.9 %all-reduce = f32[2048]{0:T(1024)S(1)} all-reduce(f32[2048]{0:T(1024)S(1)} %bitcast.61), channel_id=2, replica_groups=mesh['col'=8,'lev'=4] {'lev'}, use_global_device_ids=true, to_apply=%region_4.5.clone | all-reduce | flops 2048 | bytes 16384
  200.6 0.0 copy-done.5
  200.7 0.0 copy-done.6
  200.7 0.1 fusion.3
  200.7 0.0 copy-done.7
  200.7 0.0 copy-start.4
  200.8 0.1 select_reduce_fusion.1
  200.9 40.3 %psum.7 = f32[32]{0:T(128)} all-reduce(f32[32]{0:T(128)S(1)} %select_reduce_fusion.1), channel_id=1, replica_groups=mesh['col'=8,'lev'=4] {'col','lev'}, use_global_device_ids=true, to_apply=%region_6.7 | all-reduce | flops 32 | bytes 256 | tf_op jit(solution)/shard_map/psum | solution.py:68
  241.2 0.0 copy-done.4
  (14 shorter events, 0.1 us)
Async XLA Ops:
  0.6 8.1 %copy-start.2 = (f32[12,1024]{1,0:T(8,128)S(1)}, f32[12,1024]{1,0:T(8,128)}, u32[]{:S(2)}) copy-start(f32[12,1024]{1,0:T(8,128)} %param.11) | copy-start | bytes 147460
  0.6 42.9 %copy-start = (s32[32,2048]{1,0:T(8,128)S(1)}, s32[32,2048]{1,0:T(8,128)}, u32[]{:S(2)}) copy-start(s32[32,2048]{1,0:T(8,128)} %param.14) | copy-start | bytes 786436
  4.4 39.4 %copy-start.1 = (f32[32,2048]{1,0:T(8,128)S(1)}, f32[32,2048]{1,0:T(8,128)}, u32[]{:S(2)}) copy-start(f32[32,2048]{1,0:T(8,128)} %param.13) | copy-start | bytes 786436
  4.4 39.6 %copy-start.3 = (bf16[16,2048]{1,0:T(8,128)(2,1)S(1)}, bf16[16,2048]{1,0:T(8,128)(2,1)}, u32[]{:S(2)}) copy-start(bf16[16,2048]{1,0:T(8,128)(2,1)} %param.12) | copy-start | bytes 196612
  4.4 39.7 %copy-start.8 = (u32[32]{0:T(128)S(1)}, u32[32]{0:T(128)}, u32[]{:S(2)}) copy-start(u32[32]{0:T(128)} %constant.27) | copy-start | bytes 388
  4.4 32.3 %all-to-all-start = ((bf16[12,64,1024]{2,0,1:T(8,128)(2,1)}), bf16[12,64,1024]{2,0,1:T(8,128)(2,1)S(1)}, u32[]{:S(2)}, u32[]{:S(2)}) async-start(bf16[12,64,1024]{2,0,1:T(8,128)(2,1)} %copy.23), calls=%async_computation | async-start | bytes 4194304 | tf_op jit(solution)/shard_map/all_to_all | solution.py:42
  38.0 7.3 %collective-permute-start = (f32[16,1024]{1,0:T(8,128)S(1)}, f32[16,1024]{1,0:T(8,128)S(1)}, u32[]{:S(2)}, u32[]{:S(2)}) collective-permute-start(f32[16,1024]{1,0:T(8,128)S(1)} %bitcast.55), channel_id=1, source_target_pairs={{0,4},{4,8},{8,12},{12,16},{16,20},{20,24},{24,28},{1,5},{5,9},{9,... | collective-permute-start | bytes 196616 | tf_op jit(solution)/shard_map/ppermute | solution.py:19
  42.3 6.2 %collective-permute-start.1 = (f32[16,1024]{1,0:T(8,128)S(1)}, f32[16,1024]{1,0:T(8,128)S(1)}, u32[]{:S(2)}, u32[]{:S(2)}) collective-permute-start(f32[16,1024]{1,0:T(8,128)S(1)} %bitcast.56), channel_id=1, source_target_pairs={{4,0},{8,4},{12,8},{16,12},{20,16},{24,20},{28,24},{5,1},{9,5},{13... | collective-permute-start | bytes 196616 | tf_op jit(solution)/shard_map/ppermute | solution.py:21
  48.4 152.2 %copy-start.5 = (f32[512]{0:T(512)S(1)}, f32[512]{0:T(512)}, u32[]{:S(2)}) copy-start(f32[512]{0:T(512)} %param.15) | copy-start | bytes 6148
  48.4 152.2 %copy-start.6 = (s32[512]{0:T(512)S(1)}, s32[512]{0:T(512)}, u32[]{:S(2)}) copy-start(s32[512]{0:T(512)} %param.17) | copy-start | bytes 6148
  48.5 152.3 %copy-start.7 = (s32[512]{0:T(512)S(1)}, s32[512]{0:T(512)}, u32[]{:S(2)}) copy-start(s32[512]{0:T(512)} %param.16) | copy-start | bytes 6148
  200.7 40.4 %copy-start.4 = (f32[512]{0:T(512)}, f32[512]{0:T(512)S(1)}, u32[]{:S(2)}) copy-start(f32[512]{0:T(512)S(1)} %fusion.3) | copy-start | bytes 6148
where the time goes:
time: 242 us; the launch traced here: 241 us
  other arithmetic  124 us (51%)
  blocking collectives  74.1 us (31%)
  matrix products  21.7 us (9%)
  starting transfers between devices  9.9 us (4%)
  local copies, waits for them, and re-layouts  6.36 us (3%)
  waiting for transfers between devices  3.13 us (1%)
    reduce_sum x4, other arithmetic, block_pairs(): jnp.sum(jnp.where(index[:, None, :] == column_ids[None, :, :], weight[:,...  124 us
    psum x1, blocking collectives, shards(): type_impact = lax.psum(type_part, ('col', 'lev'))  40.3 us
    all_gather x1, blocking collectives, shards(): all_error = lax.all_gather(error_sum, 'lev', axis=0, tiled=True)  27.9 us
    dot_general x4, matrix products, block_pairs(): jnp.dot(extended, table, precision=lax.Precision.HIGHEST, preferred_eleme...  21.7 us
    unnamed x1, blocking collectives  5.87 us
    unnamed x23, local copies, waits for them, and re-layouts  5.23 us
  transfers between devices with their start and end apart: 3, of which 1 were waited for; matrix products, arithmetic and copies ran while one was open for 0% of the time, Pallas kernels for 0%

commit v1 on v0

--- a/solution.py
+++ b/solution.py
@@ -3,9 +3,13 @@
 import jax.numpy as jnp
 from jax import lax
 from jax.sharding import PartitionSpec as P
+from jax.lax import psum
 
 MEMBERS = 64
 NTYPE = 32
+produce_meshes = lambda arr_in, net_axis, row_axis: psum(
+    psum(arr_in, axis_name=net_axis), axis_name=row_axis
+)
 
 
 def with_halo(cells, sides, width):
@@ -65,7 +69,7 @@
     impact = pair * innovation * live.astype(jnp.float32) / (MEMBERS - 1.0)
     onehot = (obs_type[None, :] == jnp.arange(NTYPE, dtype=jnp.int32)[:, None]).astype(jnp.float32)
     type_part = jnp.sum(onehot * impact[None, :], axis=1)
-    type_impact = lax.psum(type_part, ("col", "lev"))
+    type_impact = produce_meshes(type_part, "lev", "col")
     return (impact, type_impact)
 
 

time: 242 us -> 227 us (0.938)
  blocking collectives: 74.1 us -> 59.8 us
    psum x1 -> x2, blocking collectives: 40.3 us -> 26.1 us  [the longest x1 20.2 us: psum(psum(arr_in, axis_name=net_axis), axis_name=row_axis)]
where the time goes in v1:
time: 227 us
  other arithmetic  124 us (55%)
  blocking collectives  59.8 us (26%)
  matrix products  21.7 us (10%)
  starting transfers between devices  9.9 us (4%)
  local copies, waits for them, and re-layouts  6.36 us (3%)
  waiting for transfers between devices  3.13 us (1%)
    reduce_sum x4, other arithmetic, block_pairs(): jnp.sum(jnp.where(index[:, None, :] == column_ids[None, :, :], weight[:,...  124 us
    all_gather x1, blocking collectives, shards(): all_error = lax.all_gather(error_sum, 'lev', axis=0, tiled=True)  27.9 us
    dot_general x4, matrix products, block_pairs(): jnp.dot(extended, table, precision=lax.Precision.HIGHEST, preferred_eleme...  21.7 us
    psum x1, blocking collectives, psum(psum(arr_in, axis_name=net_axis), axis_name=row_axis)  20.2 us
    unnamed x1, blocking collectives  5.87 us
    psum x1, blocking collectives, psum(arr_in, axis_name=net_axis)  5.81 us
    unnamed x23, local copies, waits for them, and re-layouts  5.23 us
  transfers between devices with their start and end apart: 3, of which 1 were waited for; matrix products, arithmetic and copies ran while one was open for 0% of the time, Pallas kernels for 0%

profile of v1, /device:TPU:0, one launch (start us, length us, event | category | flops | bytes accessed | tf_op | source)
XLA Modules:
  0.0 226.9 jit_solution(17100901206780303438)
XLA Ops:
  0.6 0.0 copy-start.2
  0.6 0.0 copy-start
  0.6 3.7 %copy.23 = bf16[12,64,1024]{2,0,1:T(8,128)(2,1)} copy(bf16[12,64,1024]{2,1,0:T(8,128)(2,1)} %param.10) | data formatting | bytes 3145728 | tf_op args[0]
  4.4 0.0 copy-start.1
  4.4 0.0 copy-start.3
  4.4 0.0 copy-start.8
  4.4 4.4 %all-to-all-start = ((bf16[12,64,1024]{2,0,1:T(8,128)(2,1)}), bf16[12,64,1024]{2,0,1:T(8,128)(2,1)S(1)}, u32[]{:S(2)}, u32[]{:S(2)}) async-start(bf16[12,64,1024]{2,0,1:T(8,128)(2,1)} %copy.23), calls=%async_computation | async-start | bytes 4194304 | tf_op jit(solution)/shard_map/all_to_all | solution.py:46
  8.7 0.0 copy-done.2
  8.7 27.9 %all-gather = f32[4,12,1024]{2,1,0:T(8,128)S(1)} all-gather(f32[1,12,1024]{2,1,0:T(8,128)S(1)} %bitcast.60), channel_id=1, replica_groups=mesh['col'=8,'lev'=4] {'lev'}, dimensions={0}, use_global_device_ids=true | all-gather | bytes 245760 | tf_op jit(solution)/shard_map/all_gather | solution.py:47
  36.7 0.0 all-to-all-done
  36.7 0.9 copy.36
  37.6 0.4 multiply_reduce_fusion
  38.0 4.2 %collective-permute-start = (f32[16,1024]{1,0:T(8,128)S(1)}, f32[16,1024]{1,0:T(8,128)S(1)}, u32[]{:S(2)}, u32[]{:S(2)}) collective-permute-start(f32[16,1024]{1,0:T(8,128)S(1)} %bitcast.55), channel_id=1, source_target_pairs={{0,4},{4,8},{8,12},{12,16},{16,20},{20,24},{24,28},{1,5},{5,9},{9,... | collective-permute-start | bytes 196616 | tf_op jit(solution)/shard_map/ppermute | solution.py:23
  42.3 1.3 collective-permute-start.1
  43.6 0.0 copy-done
  43.6 0.2 reshape.25
  43.8 0.0 copy-done.1
  43.8 0.2 reshape.26
  43.9 0.0 copy-done.3
  44.0 0.0 copy-done.8
  44.0 0.6 dynamic-slice
  45.3 0.0 collective-permute-done
  45.3 3.1 %collective-permute-done.1 = f32[16,1024]{1,0:T(8,128)S(1)} collective-permute-done((f32[16,1024]{1,0:T(8,128)S(1)}, f32[16,1024]{1,0:T(8,128)S(1)}, u32[]{:S(2)}, u32[]{:S(2)}) %collective-permute-start.1) | collective-permute-done | bytes 65568 | tf_op jit(solution)/shard_map/ppermute | solution.py:25
  48.4 0.0 copy-start.5
  48.4 0.0 copy-start.6
  48.5 0.0 copy-start.7
  48.5 146.3 %while.10 = (s32[]{:T(128)}, f32[4,512]{1,0:T(4,128)S(1)}, bf16[4,16,512]{2,1,0:T(8,128)(2,1)S(1)}, s32[4,32,512]{2,0,1:T(4,128)S(1)}, f32[4,32,512]{2,0,1:T(4,1...) while((s32[]{:T(128)}, f32[4,512]{1,0:T(4,128)S(1)}, bf16[4,16,512]{2,1,0:T(8,128)(2,1)S(1)}, ...), condition=%wide.region_3.4_spmd, body=%wide.region_0.3_spmd.sunk | while | flops 451436032 | bytes 13457509 | solution.py:67
  48.5 0.1 constant_dynamic-slice_fusion.4
  48.6 0.1 constant_dynamic-slice_fusion.5
  48.6 30.9 %select_reduce_fusion.3 = f32[3072,512]{1,0:T(8,128)} fusion(f32[32,512]{1,0:T(8,128)S(1)} %bitcast.50, s32[32,512]{1,0:T(8,128)S(1)} %bitcast.51), kind=kLoop, calls=%fused_computation.clone.1 | loop fusion | flops 149422080 | bytes 6422528 | tf_op jit(solution)/shard_map/while/body/eval_jaxpr/reduce_sum | solution.py:35
  79.6 5.4 %fusion.11 = f32[512]{0:T(512)S(1)} fusion(f32[3072,512]{1,0:T(8,128)} %select_reduce_fusion.3, f32[16,3072]{1,0:T(8,128)S(1)} %get-tuple-element.129, bf16[4,16,512]{2,1,0:T(8,128)(2,1)S(1)} %get-tuple-element.126, s32[]{:T(128)} %get-tuple-element.116), kind=kOutput, calls=%fused_computation.4.clone.1 | convolution fusion | flops 302013952 | bytes 6506500 | tf_op jit(solution)/shard_map/while/body/eval_jaxpr/dot_general | solution.py:38
  85.0 0.1 dynamic_update_slice.5
  85.0 0.1 constant_dynamic-slice_fusion.4
  85.1 0.1 constant_dynamic-slice_fusion.5
  85.2 30.9 %select_reduce_fusion.3 = f32[3072,512]{1,0:T(8,128)} fusion(f32[32,512]{1,0:T(8,128)S(1)} %bitcast.50, s32[32,512]{1,0:T(8,128)S(1)} %bitcast.51), kind=kLoop, calls=%fused_computation.clone.1 | loop fusion | flops 149422080 | bytes 6422528 | tf_op jit(solution)/shard_map/while/body/eval_jaxpr/reduce_sum | solution.py:35
  116.1 5.4 %fusion.11 = f32[512]{0:T(512)S(1)} fusion(f32[3072,512]{1,0:T(8,128)} %select_reduce_fusion.3, f32[16,3072]{1,0:T(8,128)S(1)} %get-tuple-element.129, bf16[4,16,512]{2,1,0:T(8,128)(2,1)S(1)} %get-tuple-element.126, s32[]{:T(128)} %get-tuple-element.116), kind=kOutput, calls=%fused_computation.4.clone.1 | convolution fusion | flops 302013952 | bytes 6506500 | tf_op jit(solution)/shard_map/while/body/eval_jaxpr/dot_general | solution.py:38
  121.5 0.1 dynamic_update_slice.5
  121.6 0.1 constant_dynamic-slice_fusion.4
  121.7 0.1 constant_dynamic-slice_fusion.5
  121.8 30.9 %select_reduce_fusion.3 = f32[3072,512]{1,0:T(8,128)} fusion(f32[32,512]{1,0:T(8,128)S(1)} %bitcast.50, s32[32,512]{1,0:T(8,128)S(1)} %bitcast.51), kind=kLoop, calls=%fused_computation.clone.1 | loop fusion | flops 149422080 | bytes 6422528 | tf_op jit(solution)/shard_map/while/body/eval_jaxpr/reduce_sum | solution.py:35
  152.7 5.4 %fusion.11 = f32[512]{0:T(512)S(1)} fusion(f32[3072,512]{1,0:T(8,128)} %select_reduce_fusion.3, f32[16,3072]{1,0:T(8,128)S(1)} %get-tuple-element.129, bf16[4,16,512]{2,1,0:T(8,128)(2,1)S(1)} %get-tuple-element.126, s32[]{:T(128)} %get-tuple-element.116), kind=kOutput, calls=%fused_computation.4.clone.1 | convolution fusion | flops 302013952 | bytes 6506500 | tf_op jit(solution)/shard_map/while/body/eval_jaxpr/dot_general | solution.py:38
  158.1 0.1 dynamic_update_slice.5
  158.2 0.1 constant_dynamic-slice_fusion.4
  158.3 0.1 constant_dynamic-slice_fusion.5
  158.4 30.9 %select_reduce_fusion.3 = f32[3072,512]{1,0:T(8,128)} fusion(f32[32,512]{1,0:T(8,128)S(1)} %bitcast.50, s32[32,512]{1,0:T(8,128)S(1)} %bitcast.51), kind=kLoop, calls=%fused_computation.clone.1 | loop fusion | flops 149422080 | bytes 6422528 | tf_op jit(solution)/shard_map/while/body/eval_jaxpr/reduce_sum | solution.py:35
  189.3 5.4 %fusion.11 = f32[512]{0:T(512)S(1)} fusion(f32[3072,512]{1,0:T(8,128)} %select_reduce_fusion.3, f32[16,3072]{1,0:T(8,128)S(1)} %get-tuple-element.129, bf16[4,16,512]{2,1,0:T(8,128)(2,1)S(1)} %get-tuple-element.126, s32[]{:T(128)} %get-tuple-element.116), kind=kOutput, calls=%fused_computation.4.clone.1 | convolution fusion | flops 302013952 | bytes 6506500 | tf_op jit(solution)/shard_map/while/body/eval_jaxpr/dot_general | solution.py:38
  194.7 0.1 dynamic_update_slice.5
  194.8 5.9 %all-reduce = f32[2048]{0:T(1024)S(1)} all-reduce(f32[2048]{0:T(1024)S(1)} %bitcast.61), channel_id=2, replica_groups=mesh['col'=8,'lev'=4] {'lev'}, use_global_device_ids=true, to_apply=%region_4.5.clone | all-reduce | flops 2048 | bytes 16384
  200.6 0.0 copy-done.5
  200.7 0.0 copy-done.6
  200.7 0.1 fusion.3
  200.7 0.0 copy-done.7
  200.7 0.0 copy-start.4
  200.8 0.1 select_reduce_fusion.1
  200.9 5.8 %psum.14 = f32[32]{0:T(128)S(1)} all-reduce(f32[32]{0:T(128)S(1)} %select_reduce_fusion.1), channel_id=1, replica_groups=mesh['col'=8,'lev'=4] {'lev'}, use_global_device_ids=true, to_apply=%region_6.7 | all-reduce | flops 32 | bytes 256 | tf_op jit(solution)/shard_map/psum | solution.py:11
  206.7 20.2 %psum.15 = f32[32]{0:T(128)} all-reduce(f32[32]{0:T(128)S(1)} %psum.14), channel_id=1, replica_groups=mesh['col'=8,'lev'=4] {'col'}, use_global_device_ids=true, to_apply=%region_7.8 | all-reduce | flops 32 | bytes 256 | tf_op jit(solution)/shard_map/psum | solution.py:10
  226.9 0.0 copy-done.4
  (14 shorter events, 0.1 us)
Async XLA Ops:
  0.6 8.1 %copy-start.2 = (f32[12,1024]{1,0:T(8,128)S(1)}, f32[12,1024]{1,0:T(8,128)}, u32[]{:S(2)}) copy-start(f32[12,1024]{1,0:T(8,128)} %param.11) | copy-start | bytes 147460
  0.6 42.9 %copy-start = (s32[32,2048]{1,0:T(8,128)S(1)}, s32[32,2048]{1,0:T(8,128)}, u32[]{:S(2)}) copy-start(s32[32,2048]{1,0:T(8,128)} %param.14) | copy-start | bytes 786436
  4.4 39.4 %copy-start.1 = (f32[32,2048]{1,0:T(8,128)S(1)}, f32[32,2048]{1,0:T(8,128)}, u32[]{:S(2)}) copy-start(f32[32,2048]{1,0:T(8,128)} %param.13) | copy-start | bytes 786436
  4.4 39.6 %copy-start.3 = (bf16[16,2048]{1,0:T(8,128)(2,1)S(1)}, bf16[16,2048]{1,0:T(8,128)(2,1)}, u32[]{:S(2)}) copy-start(bf16[16,2048]{1,0:T(8,128)(2,1)} %param.12) | copy-start | bytes 196612
  4.4 39.7 %copy-start.8 = (u32[32]{0:T(128)S(1)}, u32[32]{0:T(128)}, u32[]{:S(2)}) copy-start(u32[32]{0:T(128)} %constant.27) | copy-start | bytes 388
  4.4 32.3 %all-to-all-start = ((bf16[12,64,1024]{2,0,1:T(8,128)(2,1)}), bf16[12,64,1024]{2,0,1:T(8,128)(2,1)S(1)}, u32[]{:S(2)}, u32[]{:S(2)}) async-start(bf16[12,64,1024]{2,0,1:T(8,128)(2,1)} %copy.23), calls=%async_computation | async-start | bytes 4194304 | tf_op jit(solution)/shard_map/all_to_all | solution.py:46
  38.0 7.3 %collective-permute-start = (f32[16,1024]{1,0:T(8,128)S(1)}, f32[16,1024]{1,0:T(8,128)S(1)}, u32[]{:S(2)}, u32[]{:S(2)}) collective-permute-start(f32[16,1024]{1,0:T(8,128)S(1)} %bitcast.55), channel_id=1, source_target_pairs={{0,4},{4,8},{8,12},{12,16},{16,20},{20,24},{24,28},{1,5},{5,9},{9,... | collective-permute-start | bytes 196616 | tf_op jit(solution)/shard_map/ppermute | solution.py:23
  42.3 6.2 %collective-permute-start.1 = (f32[16,1024]{1,0:T(8,128)S(1)}, f32[16,1024]{1,0:T(8,128)S(1)}, u32[]{:S(2)}, u32[]{:S(2)}) collective-permute-start(f32[16,1024]{1,0:T(8,128)S(1)} %bitcast.56), channel_id=1, source_target_pairs={{4,0},{8,4},{12,8},{16,12},{20,16},{24,20},{28,24},{5,1},{9,5},{13... | collective-permute-start | bytes 196616 | tf_op jit(solution)/shard_map/ppermute | solution.py:25
  48.4 152.2 %copy-start.5 = (f32[512]{0:T(512)S(1)}, f32[512]{0:T(512)}, u32[]{:S(2)}) copy-start(f32[512]{0:T(512)} %param.15) | copy-start | bytes 6148
  48.4 152.2 %copy-start.6 = (s32[512]{0:T(512)S(1)}, s32[512]{0:T(512)}, u32[]{:S(2)}) copy-start(s32[512]{0:T(512)} %param.17) | copy-start | bytes 6148
  48.5 152.3 %copy-start.7 = (s32[512]{0:T(512)S(1)}, s32[512]{0:T(512)}, u32[]{:S(2)}) copy-start(s32[512]{0:T(512)} %param.16) | copy-start | bytes 6148
  200.7 26.2 %copy-start.4 = (f32[512]{0:T(512)}, f32[512]{0:T(512)S(1)}, u32[]{:S(2)}) copy-start(f32[512]{0:T(512)S(1)} %fusion.3) | copy-start | bytes 6148
